TPU v7x, 768 devices: a whole 4x8x12 slice. The times are simulated.
768 devices in a mesh: grp: 24 (over z, core), ep: 32 (over y, x).
Axes of the slice: x: 4, y: 8, z: 12, core: 2. Of those that a mesh axis runs over, the one named last changes fastest.
Arguments:
- tokens: bfloat16 [12288, 4096], P('grp', 'ep'), may hold values from -6 to 6
- grad_out: bfloat16 [12288, 4096], P('grp', 'ep'), may hold values from -1.5 to 1.5
- routes: int32 [12288, 2], P('grp'), may hold values from 0 to 11, as said below
- route_weights: float32 [12288, 2], P('grp'), may hold values from 0.1 to 1
- gate_weight: bfloat16 [24, 384, 4096], P('grp'), may hold values from -0.09375 to 0.09375
- up_weight: bfloat16 [24, 384, 4096], P('grp'), may hold values from -0.09375 to 0.09375
- down_weight: bfloat16 [24, 384, 4096], P('grp'), may hold values from -0.21875 to 0.21875
Outputs:
- grad_tokens: bfloat16 [12288, 4096], P('grp', 'ep')
- grad_gates: float32 [12288, 2], P('grp')
Inputs may be any that keep to these rules, and one draw needn't show every extreme that they name: The 2 routes of a token name different experts. Among the routes of the 512 tokens of one group, no expert is named more than 128 times; in every draw one expert is named exactly 128 times in every group.
All inputs are finite; a program needn't handle non-finite values.
Results may differ from a plain program's by a relative error of at most 0.0065.
Values may be sent and summed in bfloat16 or wider, within the bound.
A program may use at most 64 MiB of HBM per device.

v0:
```python
import jax
import jax.numpy as jnp
from jax import lax
from jax.sharding import PartitionSpec as P

TOP = 2


def from_behind(value, axis, steps):
    count = lax.axis_size(axis)
    pairs = [(source, (source + steps) % count) for source in range(count)]
    return lax.ppermute(value, axis, pairs)


def half_terms(rows_in, rows_back, gate_half, up_half, down_half):
    contract = (((1,), (1,)), ((), ()))
    gate_pre = lax.dot_general(rows_in, gate_half, contract, preferred_element_type=jnp.float32)
    up_pre = lax.dot_general(rows_in, up_half, contract, preferred_element_type=jnp.float32)
    back_proj = lax.dot_general(rows_back, down_half, contract, preferred_element_type=jnp.float32)
    sigmoid_gate = jax.nn.sigmoid(gate_pre)
    active = gate_pre * sigmoid_gate
    hidden = (active * up_pre).astype(jnp.bfloat16)
    hidden = lax.optimization_barrier(hidden)
    inner_sum = jnp.sum(hidden.astype(jnp.float32) * back_proj, axis=1)
    grad_gate_pre = (
        back_proj * up_pre * sigmoid_gate * (1.0 + gate_pre * (1.0 - sigmoid_gate))
    ).astype(jnp.bfloat16)
    grad_up_pre = (back_proj * active).astype(jnp.bfloat16)
    partial_value = jnp.dot(grad_gate_pre, gate_half, preferred_element_type=jnp.float32)
    partial_value = partial_value + jnp.dot(
        grad_up_pre, up_half, preferred_element_type=jnp.float32
    )
    return (inner_sum, partial_value.astype(jnp.bfloat16))


def on_device(tokens, grad_out, routes, route_weights, gate_weight, up_weight, down_weight):
    group_count = lax.axis_size("grp")
    rank_count = lax.axis_size("ep")
    pair_count = group_count // 2
    local_rank = lax.axis_index("ep")
    group_tokens, feat_width = tokens.shape
    full_width = feat_width * rank_count
    per_device = group_tokens // rank_count
    half_cap = (per_device * TOP + 2 * pair_count - 1) // (2 * pair_count)
    slot_total = group_count * rank_count * half_cap
    flat_expert = routes.reshape(-1)
    route_total = flat_expert.shape[0]
    onehot = (flat_expert[:, None] == jnp.arange(pair_count, dtype=jnp.int32)[None, :]).astype(
        jnp.int32
    )
    running = jnp.cumsum(onehot, axis=0)
    order_rank = jnp.sum((running - 1) * onehot, axis=1)
    parity = order_rank % 2
    dest_rank = order_rank // 2 % rank_count
    position = order_rank // (2 * rank_count)
    dest_group = parity * pair_count + flat_expert
    slot_index = (dest_group * rank_count + dest_rank) * half_cap + position
    source_token = (
        jnp.zeros((slot_total,), jnp.int32)
        .at[slot_index]
        .set(jnp.arange(route_total, dtype=jnp.int32) // TOP)
    )
    filled = jnp.zeros((slot_total,), jnp.bool_).at[slot_index].set(True)

    def pack_rows(values):
        picked = jnp.where(filled[:, None], values[source_token], jnp.zeros((), values.dtype))
        return picked.reshape(group_count, rank_count, half_cap, feat_width)

    send_in = pack_rows(tokens)
    send_back = pack_rows(grad_out)
    own_in, own_back = (
        lax.all_to_all(
            lax.all_to_all(send_in, "grp", split_axis=0, concat_axis=0, tiled=True),
            "ep",
            split_axis=1,
            concat_axis=3,
            tiled=True,
        ),
        lax.all_to_all(
            lax.all_to_all(send_back, "grp", split_axis=0, concat_axis=0, tiled=True),
            "ep",
            split_axis=1,
            concat_axis=3,
            tiled=True,
        ),
    )
    other_in, other_back = from_behind((own_in, own_back), "grp", pair_count)
    rows_in = jnp.concatenate(
        [own_in.reshape(-1, full_width), other_in.reshape(-1, full_width)], axis=0
    )
    rows_back = jnp.concatenate(
        [own_back.reshape(-1, full_width), other_back.reshape(-1, full_width)], axis=0
    )
    inner_sum, partial_value = half_terms(
        rows_in, rows_back, gate_weight[0], up_weight[0], down_weight[0]
    )
    half_rows = group_count * half_cap
    own_part = partial_value[:half_rows].reshape(group_count, 1, half_cap, full_width)
    other_part = partial_value[half_rows:].reshape(group_count, 1, half_cap, full_width)
    own_inner = inner_sum[:half_rows].reshape(group_count, half_cap)
    other_inner = inner_sum[half_rows:].reshape(group_count, half_cap)
    returned = from_behind(other_part, "grp", pair_count)
    pair_sum = (own_part.astype(jnp.float32) + returned.astype(jnp.float32)).astype(jnp.bfloat16)
    arrived = lax.all_to_all(
        lax.all_to_all(pair_sum, "grp", split_axis=0, concat_axis=0, tiled=True),
        "ep",
        split_axis=3,
        concat_axis=1,
        tiled=True,
    )
    summed = arrived.astype(jnp.float32)
    inner_first, inner_second = (
        lax.all_to_all(own_inner, "grp", split_axis=0, concat_axis=0, tiled=True),
        lax.all_to_all(other_inner, "grp", split_axis=0, concat_axis=0, tiled=True),
    )
    inner_total = inner_first + jnp.roll(inner_second, pair_count, axis=0)
    per_route = summed.reshape(slot_total, feat_width)[slot_index]
    weighted = per_route.reshape(group_tokens, TOP, feat_width) * route_weights[:, :, None]
    grad_tokens = jnp.sum(weighted, axis=1).astype(jnp.bfloat16)
    on_rank = dest_rank == local_rank
    gate_part = jnp.where(on_rank, inner_total[dest_group, position], jnp.zeros((), jnp.float32))
    grad_gates = lax.psum(gate_part.reshape(group_tokens, TOP), "ep")
    return (grad_tokens, grad_gates)


def solution(mesh):
    placed = (
        P("grp", "ep"),
        P("grp", "ep"),
        P("grp", None),
        P("grp", None),
        P("grp", None, None),
        P("grp", None, None),
        P("grp", None, None),
    )
    return jax.shard_map(
        on_device,
        mesh=mesh,
        in_specs=placed,
        out_specs=(P("grp", "ep"), P("grp", None)),
        check_vma=False,
    )
```

profile of v0, /device:TPU:64, one launch (start us, length us, event | category | flops | bytes accessed | tf_op | source)
XLA Modules:
  0.0 464.3 jit_solution(8224954506786662857)
XLA Ops:
  0.7 1.7 copy.123
  2.4 1.1 eq.39
  3.5 1.1 eq.35
  4.6 1.1 reshape.307
  5.7 3.4 reduce-window.6
  9.7 4.3 scatter_custom_fusion.1
  14.1 4.1 gather_fusion
  18.2 4.0 gather_fusion.1
  22.2 4.3 scatter_custom_fusion
  27.0 3.9 broadcast_select_fusion.1
  30.8 31.7 %all_to_all.81 = bf16[24,32,2,128]{3,2,1,0:T(2,128)(2,1)} all-to-all(bf16[24,32,2,128]{3,2,1,0:T(2,128)(2,1)S(1)} %get-tuple-element.20), channel_id=1, replica_groups=mesh['grp'=24,'ep'=32] {'grp'}, dimensions={0} | all-to-all | bytes 786432 | tf_op jit(solution)/shard_map/all_to_all | solution.py:73
  62.6 7.4 %all-to-all-start = ((bf16[24,32,2,128]{3,2,1,0:T(2,128)(2,1)}), bf16[24,32,2,128]{3,2,1,0:T(2,128)(2,1)S(1)}, u32[]{:S(2)}, u32[]{:S(2)}) async-start(bf16[24,32,2,128]{3,2,1,0:T(2,128)(2,1)} %get-tuple-element.19), calls=%async_computation | async-start | bytes 786432 | tf_op jit(solution)/shard_map/all_to_all | solution.py:80
  70.0 2.0 copy.132
  72.0 15.2 %all-to-all-done = bf16[24,32,2,128]{3,2,1,0:T(2,128)(2,1)S(1)} async-done(((bf16[24,32,2,128]{3,2,1,0:T(2,128)(2,1)}), bf16[24,32,2,128]{3,2,1,0:T(2,128)(2,1)S(1)}, u32[]{:S(2)}, u32[]{:S(2)}) %all-to-all-start) | async-done | bytes 393248 | tf_op jit(solution)/shard_map/all_to_all | solution.py:80
  87.9 9.9 %all-to-all-start.3 = ((bf16[24,32,2,128]{3,2,0,1:T(2,128)(2,1)}), bf16[24,32,2,128]{3,2,0,1:T(2,128)(2,1)S(1)}, u32[]{:S(2)}, u32[]{:S(2)}) async-start(bf16[24,32,2,128]{3,2,0,1:T(2,128)(2,1)} %copy.132), calls=%async_computation.3 | async-start | bytes 786432 | tf_op jit(solution)/shard_map/all_to_all | solution.py:72
  97.9 2.0 copy.128
  99.9 13.9 %all-to-all-done.3 = bf16[24,32,2,128]{3,2,0,1:T(2,128)(2,1)S(1)} async-done(((bf16[24,32,2,128]{3,2,0,1:T(2,128)(2,1)}), bf16[24,32,2,128]{3,2,0,1:T(2,128)(2,1)S(1)}, u32[]{:S(2)}, u32[]{:S(2)}) %all-to-all-start.3) | async-done | bytes 393248 | tf_op jit(solution)/shard_map/all_to_all | solution.py:72
  114.6 5.0 %all-to-all-start.1 = ((bf16[24,32,2,128]{3,2,0,1:T(2,128)(2,1)}), bf16[24,32,2,128]{3,2,0,1:T(2,128)(2,1)S(1)}, u32[]{:S(2)}, u32[]{:S(2)}) async-start(bf16[24,32,2,128]{3,2,0,1:T(2,128)(2,1)} %copy.128), calls=%async_computation.1 | async-start | bytes 786432 | tf_op jit(solution)/shard_map/all_to_all | solution.py:79
  119.6 1.8 copy.134
  121.4 1.8 copy.133
  123.2 1.9 all_to_all.65
  125.2 4.1 collective-permute-start.1
  129.3 1.9 bitcast_dynamic-update-slice_fusion
  131.2 3.6 all-to-all-done.1
  136.6 1.9 all_to_all.60
  138.5 4.5 collective-permute-start
  143.0 1.9 copy.156
  144.9 16.4 %collective-permute-done.1 = bf16[24,1,2,4096]{3,0,2,1:T(8,128)(2,1)} collective-permute-done((bf16[24,1,2,4096]{3,0,2,1:T(8,128)(2,1)}, bf16[24,1,2,4096]{3,0,2,1:T(8,128)(2,1)}, u32[]{:S(2)}, u32[]{:S(2)}) %collective-permute-start.1) | collective-permute-done | bytes 393248 | tf_op jit(solution)/shard_map/ppermute | solution.py:12
  161.3 2.2 copy.135
  163.5 1.1 reshape.311
  165.4 3.3 fusion.3
  168.7 1.1 multiply_convert_fusion
  169.8 8.0 %collective-permute-done = bf16[24,1,2,4096]{3,0,2,1:T(8,128)(2,1)} collective-permute-done((bf16[24,1,2,4096]{3,0,2,1:T(8,128)(2,1)}, bf16[24,1,2,4096]{3,0,2,1:T(8,128)(2,1)}, u32[]{:S(2)}, u32[]{:S(2)}) %collective-permute-start) | collective-permute-done | bytes 393248 | tf_op jit(solution)/shard_map/ppermute | solution.py:12
  177.8 2.1 copy.131
  179.9 1.9 reshape.309
  181.8 3.4 multiply_reduce_fusion.1
  186.8 1.1 fusion.44
  187.9 1.3 reshape.312
  189.2 1.0 copy.136
  190.1 8.1 %collective-permute-start.2 = (bf16[24,1,2,4096]{3,0,2,1:T(8,128)(2,1)}, bf16[24,1,2,4096]{3,0,2,1:T(8,128)(2,1)S(1)}, u32[]{:S(2)}, u32[]{:S(2)}) collective-permute-start(bf16[24,1,2,4096]{3,0,2,1:T(8,128)(2,1)} %copy.136), channel_id=1, source_target_pairs={{0,384},{32,416},{64,448},{96,480},{128,512},{160,544},{192,576},{... | collective-permute-start | bytes 1179656 | tf_op jit(solution)/shard_map/ppermute | solution.py:12
  198.8 1.3 all_to_all.71
  200.1 13.1 %all-to-all-start.7 = ((f32[24,1,2]{2,1,0:T(1,128)}), f32[24,1,2]{2,1,0:T(1,128)}, u32[]{:S(2)}, u32[]{:S(2)}) async-start(f32[24,1,2]{2,1,0:T(1,128)} %bitcast.93), calls=%async_computation.7 | async-start | bytes 24576 | tf_op jit(solution)/shard_map/all_to_all | solution.py:114
  213.2 2.5 reshape.314
  215.7 1.6 fusion.13
  217.3 1.1 copy.138
  218.5 6.7 %all-to-all-done.7 = f32[24,1,2]{2,1,0:T(1,128)} async-done(((f32[24,1,2]{2,1,0:T(1,128)}), f32[24,1,2]{2,1,0:T(1,128)}, u32[]{:S(2)}, u32[]{:S(2)}) %all-to-all-start.7) | async-done | bytes 224 | tf_op jit(solution)/shard_map/all_to_all | solution.py:114
  225.2 10.0 %all-to-all-start.4 = ((bf16[24,1,2,4096]{3,2,1,0:T(2,128)(2,1)}), bf16[24,1,2,4096]{3,2,1,0:T(2,128)(2,1)S(1)}, u32[]{:S(2)}, u32[]{:S(2)}) async-start(bf16[24,1,2,4096]{3,2,1,0:T(2,128)(2,1)} %copy.138), calls=%async_computation.4 | async-start | bytes 786432 | tf_op jit(solution)/shard_map/all_to_all | solution.py:105
  235.8 16.3 %all-to-all-done.4 = bf16[24,1,2,4096]{3,2,1,0:T(2,128)(2,1)S(1)} async-done(((bf16[24,1,2,4096]{3,2,1,0:T(2,128)(2,1)}), bf16[24,1,2,4096]{3,2,1,0:T(2,128)(2,1)S(1)}, u32[]{:S(2)}, u32[]{:S(2)}) %all-to-all-start.4) | async-done | bytes 393248 | tf_op jit(solution)/shard_map/all_to_all | solution.py:105
  252.1 7.9 %all-to-all-start.6 = ((f32[24,1,2]{2,1,0:T(1,128)}), f32[24,1,2]{2,1,0:T(1,128)}, u32[]{:S(2)}, u32[]{:S(2)}) async-start(f32[24,1,2]{2,1,0:T(1,128)} %bitcast.94), calls=%async_computation.6 | async-start | bytes 24576 | tf_op jit(solution)/shard_map/all_to_all | solution.py:113
  260.0 3.8 copy.139
  263.9 7.9 %reshape.369 = bf16[32,2,3072]{2,1,0:T(2,128)(2,1)} reshape(bf16[4096,1,2,24]{3,2,1,0:T(2,128)(2,1)} %bitcast.77) | data formatting | bytes 786432
  271.8 6.6 %all-to-all-start.5 = ((bf16[32,2,3072]{2,1,0:T(2,128)(2,1)}), bf16[32,2,3072]{2,1,0:T(2,128)(2,1)S(1)}, u32[]{:S(2)}, u32[]{:S(2)}) async-start(bf16[32,2,3072]{2,1,0:T(2,128)(2,1)} %reshape.369), calls=%async_computation.5 | async-start | bytes 786432 | tf_op jit(solution)/shard_map/all_to_all | solution.py:104
  279.8 1.6 copy.141
  281.4 1.3 fusion.45
  282.7 1.3 copy.145
  286.2 8.8 %gather_fusion.3 = f32[1024]{0:T(1024)S(1)} fusion(f32[24,2]{0,1:T(2,128)S(1)} %maximum_add_fusion, s32[1024]{0:T(1024)S(1)} %bitcast.75), kind=kCustom, calls=%fused_computation.3 | custom fusion | bytes 16384 | tf_op jit(solution)/shard_map/gather | solution.py:121
  295.1 0.9 gather.24
  296.0 2.0 fusion.18
  298.0 145.6 %psum.7 = f32[512,2]{1,0:T(8,128)} all-reduce(f32[512,2]{1,0:T(8,128)} %fusion.18), channel_id=1, replica_groups=mesh['grp'=24,'ep'=32] {'ep'}, use_global_device_ids=true, to_apply=%region_7.8 | all-reduce | flops 1024 | bytes 8192 | tf_op jit(solution)/shard_map/psum | solution.py:122
  443.5 1.7 copy.147
  445.2 4.0 reshape.370
  449.1 5.6 %copy.140 = f32[24,1,2,32,128]{4,2,3,0,1:T(2,128)} copy(bf16[24,1,2,32,128]{0,2,4,3,1:T(2,128)(2,1)} %bitcast.78) | data formatting | bytes 1179648 | tf_op jit(solution)/shard_map/convert_element_type | solution.py:111
  454.8 5.2 %gather_fusion.2 = f32[1024,128]{1,0:T(8,128)} fusion(f32[1536,128]{1,0:T(8,128)} %bitcast.76, s32[1024]{0:T(1024)S(1)} %copy-done.8), kind=kCustom, calls=%fused_computation.2 | custom fusion | bytes 1052672 | tf_op jit(solution)/shard_map/gather | solution.py:117
  459.9 4.4 multiply_reduce_fusion
  (52 shorter events, 11.4 us)
Async XLA Ops:
  0.6 168.0 %copy-start = (bf16[1,384,4096]{2,1,0:T(8,128)(2,1)S(1)}, bf16[1,384,4096]{2,1,0:T(8,128)(2,1)}, u32[]{:S(2)}) copy-start(bf16[1,384,4096]{2,1,0:T(8,128)(2,1)} %param.12) | copy-start | bytes 9437188
  0.6 13.4 %copy-start.1 = (bf16[512,128]{1,0:T(8,128)(2,1)S(1)}, bf16[512,128]{1,0:T(8,128)(2,1)}, u32[]{:S(2)}) copy-start(bf16[512,128]{1,0:T(8,128)(2,1)} %param.8) | copy-start | bytes 393220
  0.7 17.5 %copy-start.2 = (bf16[512,128]{1,0:T(8,128)(2,1)S(1)}, bf16[512,128]{1,0:T(8,128)(2,1)}, u32[]{:S(2)}) copy-start(bf16[512,128]{1,0:T(8,128)(2,1)} %param.7) | copy-start | bytes 393220
  62.6 24.6 %all-to-all-start = ((bf16[24,32,2,128]{3,2,1,0:T(2,128)(2,1)}), bf16[24,32,2,128]{3,2,1,0:T(2,128)(2,1)S(1)}, u32[]{:S(2)}, u32[]{:S(2)}) async-start(bf16[24,32,2,128]{3,2,1,0:T(2,128)(2,1)} %get-tuple-element.19), calls=%async_computation | async-start | bytes 786432 | tf_op jit(solution)/shard_map/all_to_all | solution.py:80
  87.2 0.7 copy-start.6
  87.9 25.9 %all-to-all-start.3 = ((bf16[24,32,2,128]{3,2,0,1:T(2,128)(2,1)}), bf16[24,32,2,128]{3,2,0,1:T(2,128)(2,1)S(1)}, u32[]{:S(2)}, u32[]{:S(2)}) async-start(bf16[24,32,2,128]{3,2,0,1:T(2,128)(2,1)} %copy.132), calls=%async_computation.3 | async-start | bytes 786432 | tf_op jit(solution)/shard_map/all_to_all | solution.py:72
  113.8 0.8 copy-start.5
  114.6 20.2 %all-to-all-start.1 = ((bf16[24,32,2,128]{3,2,0,1:T(2,128)(2,1)}), bf16[24,32,2,128]{3,2,0,1:T(2,128)(2,1)S(1)}, u32[]{:S(2)}, u32[]{:S(2)}) async-start(bf16[24,32,2,128]{3,2,0,1:T(2,128)(2,1)} %copy.128), calls=%async_computation.1 | async-start | bytes 786432 | tf_op jit(solution)/shard_map/all_to_all | solution.py:79
  125.2 36.1 %collective-permute-start.1 = (bf16[24,1,2,4096]{3,0,2,1:T(8,128)(2,1)}, bf16[24,1,2,4096]{3,0,2,1:T(8,128)(2,1)}, u32[]{:S(2)}, u32[]{:S(2)}) collective-permute-start(bf16[24,1,2,4096]{3,0,2,1:T(8,128)(2,1)} %all_to_all.65), channel_id=1, source_target_pairs={{0,384},{32,416},{64,448},{96,480},{128,512},{160,544},{192,576},{... | collective-permute-start | bytes 1179656 | tf_op jit(solution)/shard_map/ppermute | solution.py:12
  138.5 39.3 %collective-permute-start = (bf16[24,1,2,4096]{3,0,2,1:T(8,128)(2,1)}, bf16[24,1,2,4096]{3,0,2,1:T(8,128)(2,1)}, u32[]{:S(2)}, u32[]{:S(2)}) collective-permute-start(bf16[24,1,2,4096]{3,0,2,1:T(8,128)(2,1)} %all_to_all.60), channel_id=1, source_target_pairs={{0,384},{32,416},{64,448},{96,480},{128,512},{160,544},{192,576},{... | collective-permute-start | bytes 1179656 | tf_op jit(solution)/shard_map/ppermute | solution.py:12
  165.4 3.3 copy-start.4
  181.8 3.5 copy-start.3
  190.1 25.6 %collective-permute-start.2 = (bf16[24,1,2,4096]{3,0,2,1:T(8,128)(2,1)}, bf16[24,1,2,4096]{3,0,2,1:T(8,128)(2,1)S(1)}, u32[]{:S(2)}, u32[]{:S(2)}) collective-permute-start(bf16[24,1,2,4096]{3,0,2,1:T(8,128)(2,1)} %copy.136), channel_id=1, source_target_pairs={{0,384},{32,416},{64,448},{96,480},{128,512},{160,544},{192,576},{... | collective-permute-start | bytes 1179656 | tf_op jit(solution)/shard_map/ppermute | solution.py:12
  198.8 36.3 %copy-start.9 = (f32[48]{0:T(128)S(1)}, f32[48]{0:T(128)}, u32[]{:S(2)}) copy-start(f32[48]{0:T(128)} %get-tuple-element.23) | copy-start | bytes 580
  200.1 25.1 %all-to-all-start.7 = ((f32[24,1,2]{2,1,0:T(1,128)}), f32[24,1,2]{2,1,0:T(1,128)}, u32[]{:S(2)}, u32[]{:S(2)}) async-start(f32[24,1,2]{2,1,0:T(1,128)} %bitcast.93), calls=%async_computation.7 | async-start | bytes 24576 | tf_op jit(solution)/shard_map/all_to_all | solution.py:114
  225.2 27.0 %all-to-all-start.4 = ((bf16[24,1,2,4096]{3,2,1,0:T(2,128)(2,1)}), bf16[24,1,2,4096]{3,2,1,0:T(2,128)(2,1)S(1)}, u32[]{:S(2)}, u32[]{:S(2)}) async-start(bf16[24,1,2,4096]{3,2,1,0:T(2,128)(2,1)} %copy.138), calls=%async_computation.4 | async-start | bytes 786432 | tf_op jit(solution)/shard_map/all_to_all | solution.py:105
  252.1 19.6 %all-to-all-start.6 = ((f32[24,1,2]{2,1,0:T(1,128)}), f32[24,1,2]{2,1,0:T(1,128)}, u32[]{:S(2)}, u32[]{:S(2)}) async-start(f32[24,1,2]{2,1,0:T(1,128)} %bitcast.94), calls=%async_computation.6 | async-start | bytes 24576 | tf_op jit(solution)/shard_map/all_to_all | solution.py:113
  271.8 173.4 %all-to-all-start.5 = ((bf16[32,2,3072]{2,1,0:T(2,128)(2,1)}), bf16[32,2,3072]{2,1,0:T(2,128)(2,1)S(1)}, u32[]{:S(2)}, u32[]{:S(2)}) async-start(bf16[32,2,3072]{2,1,0:T(2,128)(2,1)} %reshape.369), calls=%async_computation.5 | async-start | bytes 786432 | tf_op jit(solution)/shard_map/all_to_all | solution.py:104
  298.0 156.8 %copy-start.8 = (s32[1024]{0:T(1024)S(1)}, s32[1024]{0:T(1024)}, u32[]{:S(2)}) copy-start(s32[1024]{0:T(1024)} %broadcast_clamp_fusion) | copy-start | bytes 12292
  449.1 10.8 %copy-start.7 = (f32[512,2]{1,0:T(8,128)S(1)}, f32[512,2]{1,0:T(8,128)}, u32[]{:S(2)}) copy-start(f32[512,2]{1,0:T(8,128)} %copy.141) | copy-start | bytes 12292
where the time goes:
time: 466 us; the launch traced here: 464 us
  blocking collectives  177 us (38%)
  local copies, waits for them, and re-layouts  102 us (22%)
  waiting for transfers between devices  80.2 us (17%)
  starting transfers between devices  76.7 us (16%)
  other arithmetic  18 us (4%)
  matrix products  9.27 us (2%)
    psum x1, blocking collectives, on_device(): grad_gates = lax.psum(gate_part.reshape(group_tokens, TOP), 'ep')  146 us
    all_to_all x1, blocking collectives, on_device(): lax.all_to_all(send_in, 'grp', split_axis=0, concat_axis=0, tiled=True)  31.7 us
    ppermute x3, waiting for transfers between devices, from_behind(): return lax.ppermute(value, axis, pairs)  24.4 us
    unnamed x29, local copies, waits for them, and re-layouts  22.1 us
    ppermute x3, starting transfers between devices, from_behind(): return lax.ppermute(value, axis, pairs)  16.8 us
    all_to_all x1, waiting for transfers between devices, on_device(): lax.all_to_all(pair_sum, 'grp', split_axis=0, concat_axis=0, tiled=True)  16.3 us
    all_to_all x1, waiting for transfers between devices, on_device(): lax.all_to_all(send_back, 'grp', split_axis=0, concat_axis=0, tiled=True)  15.2 us
    all_to_all x1, waiting for transfers between devices, on_device(): lax.all_to_all(lax.all_to_all(send_in, 'grp', split_axis=0, concat_axis=0...  13.9 us
  transfers between devices with their start and end apart: 10, of which 7 were waited for; matrix products, arithmetic and copies ran while one was open for 13% of the time, Pallas kernels for 0%

commit v1 on v0

v1 whole, which is shorter than its diff:
```python
import functools

import jax
import jax.numpy as jnp
from jax import lax
from jax.experimental import pallas as pl
from jax.experimental.pallas import tpu as pltpu
from jax.sharding import PartitionSpec as P

MESH = pl.DeviceIdType.MESH
LANES = 128
NT = (((1,), (1,)), ((), ()))


def kernel(
    dims,
    tok_ref,
    grad_ref,
    routes_ref,
    rw_ref,
    gate_hbm,
    up_hbm,
    down_hbm,
    out_ref,
    gates_ref,
    xb,
    gb,
    cb,
    sb,
    rl,
    rr,
    tl,
    tr,
    fin,
    wg,
    wu,
    wd,
    gate_s,
    up_s,
    inner_out,
    inner_in,
    a_send,
    a_recv,
    g_send,
    g_recv,
    s_send,
    s_recv,
    c_send,
    c_recv,
    r_send,
    r_recv,
    e_send,
    e_recv,
    w_sem,
):
    groups, ranks, rows, width, half = dims
    chips = groups // 2
    far = chips // 2
    experts = groups // 2
    grp = lax.axis_index("grp")
    rank = lax.axis_index("ep")
    z = grp // 2
    core = lax.rem(grp, 2)
    other = 1 - core
    right = lax.rem(z + 1, chips) * 2 + core
    left = lax.rem(z + chips - 1, chips) * 2 + core
    sibling = z * 2 + other
    ahead = (right, left)
    expert = lax.rem(grp, experts)
    mid = width // 2
    parts = (pl.ds(0, mid), pl.ds(mid, width + LANES - mid))

    weights = [
        pltpu.make_async_copy(src.at[0], dst, w_sem.at[i])
        for i, (src, dst) in enumerate(((gate_hbm, wg), (up_hbm, wu), (down_hbm, wd)))
    ]
    for copy in weights:
        copy.start()

    barrier = pltpu.get_barrier_semaphore()
    for peer in (right, left, sibling):
        pl.semaphore_signal(barrier, inc=1, device_id=(peer, rank), device_id_type=MESH)

    def greet(i, carry):
        pl.semaphore_signal(
            barrier, inc=1, device_id=(grp, lax.rem(rank + i, ranks)), device_id_type=MESH
        )
        return carry

    lax.fori_loop(1, ranks, greet, 0)

    token_lane = lax.broadcasted_iota(jnp.int32, (rows, rows * ranks), 1)
    token_row = lax.broadcasted_iota(jnp.int32, (rows, rows * ranks), 0)
    mine = token_lane == token_row + rank * rows
    lane = lax.broadcasted_iota(jnp.int32, (rows, LANES), 1)

    def column(values, k):
        return jnp.sum(jnp.where(mine, values[k : k + 1, :], 0.0), axis=1, keepdims=True)

    routes_f = routes_ref[...].astype(jnp.float32)
    rw_f = rw_ref[...]
    lane_f = lane.astype(jnp.float32)
    meta = jnp.zeros((rows, LANES), jnp.float32)
    for k in range(2):
        chosen = column(routes_f, k)
        weight = column(rw_f, k)
        high = weight.astype(jnp.bfloat16).astype(jnp.float32)
        low = weight - high
        meta = meta + jnp.where(lane_f == chosen, high, 0.0)
        meta = meta + jnp.where(lane_f == chosen + float(experts), low, 0.0)
    own_slot = (far, 1)
    xb[far, 1, core, :, pl.ds(width, LANES)] = meta.astype(jnp.bfloat16)
    own_rows = pl.ds(pl.multiple_of(rank * rows, rows), rows)
    own_cols = pl.ds(pl.multiple_of(rank * LANES, LANES), LANES)
    xb[far, 1, core, :, own_cols] = tok_ref[own_rows, :]
    gb[far, 1, core, :, own_cols] = grad_ref[own_rows, :]

    pl.semaphore_wait(barrier, 3 + ranks - 1)

    def enter(which, i):
        src, buf = ((tok_ref, xb), (grad_ref, gb))[which]
        peer = lax.rem(rank + i, ranks)
        return pltpu.make_async_remote_copy(
            src_ref=src.at[pl.ds(pl.multiple_of(peer * rows, rows), rows), :],
            dst_ref=buf.at[far, 1, core, :, own_cols],
            send_sem=a_send.at[which, i],
            recv_sem=a_recv.at[which, i],
            device_id=(grp, peer),
            device_id_type=MESH,
        )

    def landed(which, i):
        buf = (xb, gb)[which]
        peer = lax.rem(rank + ranks - i, ranks)
        here = buf.at[far, 1, core, :, pl.ds(pl.multiple_of(peer * LANES, LANES), LANES)]
        return pltpu.make_async_remote_copy(
            src_ref=here,
            dst_ref=here,
            send_sem=a_send.at[which, i],
            recv_sem=a_recv.at[which, i],
            device_id=(grp, peer),
            device_id_type=MESH,
        )

    for which in range(2):

        def send_in(i, carry):
            enter(which, i).start()
            return carry

        lax.fori_loop(1, ranks, send_in, 0)

    def ring(direction, which, step):
        buf = (xb, gb)[which]
        if isinstance(step, int) and step == 0:
            src = buf.at[far, 1, core]
        else:
            src = buf.at[step, direction, core]
        return pltpu.make_async_remote_copy(
            src_ref=src,
            dst_ref=buf.at[step + 1, direction if not (isinstance(step, int) and step == far - 1) else 0, core],
            send_sem=g_send.at[direction, which, step],
            recv_sem=g_recv.at[direction, which, step + 1],
            device_id=(ahead[direction], rank),
            device_id_type=MESH,
        )

    def ring_last(direction, which):
        buf = (xb, gb)[which]
        return pltpu.make_async_remote_copy(
            src_ref=buf.at[far - 1, direction, core],
            dst_ref=buf.at[far, 0, core],
            send_sem=g_send.at[direction, which, far - 1],
            recv_sem=g_recv.at[direction, which, far],
            device_id=(ahead[direction], rank),
            device_id_type=MESH,
        )

    def share(which, slot, side):
        buf = (xb, gb)[which]
        return pltpu.make_async_remote_copy(
            src_ref=buf.at[slot, side, core],
            dst_ref=buf.at[slot, side, core],
            send_sem=s_send.at[side, which, slot],
            recv_sem=s_recv.at[side, which, slot],
            device_id=(sibling, rank),
            device_id_type=MESH,
        )

    def shared(which, slot, side):
        buf = (xb, gb)[which]
        return pltpu.make_async_remote_copy(
            src_ref=buf.at[slot, side, other],
            dst_ref=buf.at[slot, side, other],
            send_sem=s_send.at[side, which, slot],
            recv_sem=s_recv.at[side, which, slot],
            device_id=(sibling, rank),
            device_id_type=MESH,
        )

    for which in range(2):

        def arrive(i, carry):
            landed(which, i).wait_recv()
            return carry

        lax.fori_loop(1, ranks, arrive, 0)
        for direction in range(2):
            ring(direction, which, 0).start()
        share(which, far, 1).start()

    for copy in weights:
        copy.wait()

    lanes_m = lax.broadcasted_iota(jnp.int32, (4 * rows, LANES), 1)

    def first_half(slot):
        for side in range(2):
            shared(0, slot, side).wait_recv()
        x = xb[slot, :, :, :, pl.ds(0, width)].reshape(4 * rows, width)
        gate_s[...] = lax.dot_general(x, wg[...], NT, preferred_element_type=jnp.float32)
        up_s[...] = lax.dot_general(x, wu[...], NT, preferred_element_type=jnp.float32)

    def hand_over(slot, side):
        return pltpu.make_async_remote_copy(
            src_ref=cb.at[slot, side, other],
            dst_ref=sb.at[slot, side],
            send_sem=c_send.at[side, slot],
            recv_sem=c_recv.at[side, slot],
            device_id=(sibling, rank),
            device_id_type=MESH,
        )

    def second_half(slot):
        for side in range(2):
            shared(1, slot, side).wait_recv()
        gr = gb[slot].reshape(4 * rows, width)
        back = lax.dot_general(gr, wd[...], NT, preferred_element_type=jnp.float32)
        gate_pre = gate_s[...]
        up_pre = up_s[...]
        sig = jax.nn.sigmoid(gate_pre)
        active = gate_pre * sig
        hidden = (active * up_pre).astype(jnp.bfloat16).astype(jnp.float32)
        inner = jnp.sum(hidden * back, axis=1, keepdims=True)
        d_gate = (back * up_pre * sig * (1.0 + gate_pre * (1.0 - sig))).astype(jnp.bfloat16)
        d_up = (back * active).astype(jnp.bfloat16)
        info = xb[slot, :, :, :, pl.ds(width, LANES)].reshape(4 * rows, LANES).astype(jnp.float32)
        picked = (lanes_m == expert) | (lanes_m == expert + experts)
        weight = jnp.sum(jnp.where(picked, info, 0.0), axis=1, keepdims=True)
        inner = jnp.where(weight > 0.0, inner, 0.0)
        high = inner.astype(jnp.bfloat16).astype(jnp.float32)
        low = inner - high
        extra = jnp.where(lanes_m == grp, high, jnp.where(lanes_m == grp + groups, low, 0.0))
        cb[slot, :, :, :, pl.ds(width, LANES)] = extra.astype(jnp.bfloat16).reshape(
            2, 2, rows, LANES
        )
        tile = 512

        def columns(n, carry):
            cols = pl.ds(pl.multiple_of(n * tile, tile), tile)
            part = jnp.dot(d_gate, wg[:, cols], preferred_element_type=jnp.float32)
            part = part + jnp.dot(d_up, wu[:, cols], preferred_element_type=jnp.float32)
            cb[slot, :, :, :, cols] = (weight * part).astype(jnp.bfloat16).reshape(
                2, 2, rows, tile
            )
            return carry

        lax.fori_loop(0, width // tile, columns, 0)
        for side in range(2):
            hand_over(slot, side).start()

    def step(t, carry):
        for which in range(2):

            @pl.when(t < far)
            def _():
                for direction in range(2):
                    ring(direction, which, t - 1).wait_recv()
                    share(which, t, direction).start()

            @pl.when(t < far - 1)
            def _():
                for direction in range(2):
                    ring(direction, which, t).start()

            @pl.when(t == far - 1)
            def _():
                ring_last(which, which).start()

            @pl.when(t == far)
            def _():
                ring_last(which, which).wait_recv()
                share(which, far, 0).start()

            @pl.when(t > 1)
            def _():
                (first_half, second_half)[which](t - 1)

        return carry

    lax.fori_loop(1, far + 2, step, 0)

    def returning(direction, part, distance):
        stage, land = ((tl, rl), (tr, rr))[direction]
        return pltpu.make_async_remote_copy(
            src_ref=stage.at[distance, :, parts[part]],
            dst_ref=land.at[distance - 1, :, parts[part]],
            send_sem=r_send.at[direction, part, distance],
            recv_sem=r_recv.at[direction, part, distance],
            device_id=((left, right)[direction], rank),
            device_id_type=MESH,
        )

    def own_terms(slot, side, cols):
        return cb[slot, side, core, :, cols].astype(jnp.float32) + sb[slot, side, :, cols].astype(
            jnp.float32
        )

    hand_over(far, 0).wait_recv()
    for direction in range(2):
        stage = (tl, tr)[direction]
        cols = parts[direction]
        stage[far, :, cols] = own_terms(far, 0, cols).astype(jnp.bfloat16)
        returning(direction, direction, far).start()
    for distance in range(far - 1, 0, -1):
        for direction in range(2):
            hand_over(distance, direction).wait_recv()
        for nth in range(2):
            for direction in range(2):
                stage, land = ((tl, rl), (tr, rr))[direction]
                part = nth if distance < far - 1 else (nth + 1 - direction) % 2
                cols = parts[part]
                value = own_terms(distance, direction, cols)
                if distance < far - 1 or part == direction:
                    returning(direction, part, distance + 1).wait_recv()
                    value = value + land[distance, :, cols].astype(jnp.float32)
                stage[distance, :, cols] = value.astype(jnp.bfloat16)
                returning(direction, part, distance).start()

    hand_over(far, 1).wait_recv()

    def leave(i):
        peer = lax.rem(rank + i, ranks)
        return pltpu.make_async_remote_copy(
            src_ref=fin.at[:, pl.ds(pl.multiple_of(peer * LANES, LANES), LANES)],
            dst_ref=out_ref.at[own_rows, :],
            send_sem=e_send.at[0, i],
            recv_sem=e_recv.at[0, i],
            device_id=(grp, peer),
            device_id_type=MESH,
        )

    def leave_inner(i):
        peer = lax.rem(rank + i, ranks)
        return pltpu.make_async_remote_copy(
            src_ref=inner_out,
            dst_ref=inner_in.at[rank],
            send_sem=e_send.at[1, i],
            recv_sem=e_recv.at[1, i],
            device_id=(grp, peer),
            device_id_type=MESH,
        )

    def back_home(i):
        peer = lax.rem(rank + ranks - i, ranks)
        here = out_ref.at[pl.ds(pl.multiple_of(peer * rows, rows), rows), :]
        return pltpu.make_async_remote_copy(
            src_ref=here,
            dst_ref=here,
            send_sem=e_send.at[0, i],
            recv_sem=e_recv.at[0, i],
            device_id=(grp, peer),
            device_id_type=MESH,
        )

    def back_home_inner(i):
        peer = lax.rem(rank + ranks - i, ranks)
        return pltpu.make_async_remote_copy(
            src_ref=inner_out,
            dst_ref=inner_in.at[peer],
            send_sem=e_send.at[1, i],
            recv_sem=e_recv.at[1, i],
            device_id=(grp, peer),
            device_id_type=MESH,
        )

    for part in range(2):
        cols = parts[part]
        for direction in range(2):
            returning(direction, part, 1).wait_recv()
        total = (
            own_terms(far, 1, cols)
            + rl[0, :, cols].astype(jnp.float32)
            + rr[0, :, cols].astype(jnp.float32)
        )
        if part == 0:
            fin[:, pl.ds(0, mid)] = total.astype(jnp.bfloat16)
        else:
            fin[:, pl.ds(mid, width - mid)] = total[:, : width - mid].astype(jnp.bfloat16)
            inner_lanes = total[:, width - mid :]

    place = (lane == lax.rem(rank, LANES // rows) * rows + lax.broadcasted_iota(
        jnp.int32, (rows, LANES), 0
    ))
    for k in range(2):
        chosen = column(routes_f, k)
        wanted = jnp.zeros((rows, LANES), jnp.bool_)
        for piece in range(4):
            wanted = wanted | (lane_f == chosen + float(piece * experts))
        gate_grad = jnp.sum(jnp.where(wanted, inner_lanes, 0.0), axis=1, keepdims=True)
        inner_out[k : k + 1, :] = jnp.sum(jnp.where(place, gate_grad, 0.0), axis=0, keepdims=True)

    def send_out(i, carry):
        leave(i).start()
        leave_inner(i).start()
        return carry

    lax.fori_loop(1, ranks, send_out, 0)
    out_ref[own_rows, :] = fin[:, own_cols]
    inner_in[rank] = inner_out[...]

    def drain_in(i, carry):
        for which in range(2):
            enter(which, i).wait_send()
        return carry

    lax.fori_loop(1, ranks, drain_in, 0)
    for which in range(2):
        for direction in range(2):
            ring(direction, which, 0).wait_send()
        share(which, far, 0).wait_send()
        share(which, far, 1).wait_send()
        ring_last(which, which).wait_send()
        for slot in range(1, far):
            for direction in range(2):
                share(which, slot, direction).wait_send()
                if slot < far - 1:
                    ring(direction, which, slot).wait_send()
    for slot in range(1, far + 1):
        for side in range(2):
            hand_over(slot, side).wait_send()
    for direction in range(2):
        returning(direction, direction, far).wait_send()
        for part in range(2):
            for distance in range(1, far):
                returning(direction, part, distance).wait_send()

    def finish(i, carry):
        back_home(i).wait_recv()
        back_home_inner(i).wait_recv()
        leave(i).wait_send()
        leave_inner(i).wait_send()
        return carry

    lax.fori_loop(1, ranks, finish, 0)
    per = LANES // rows
    for q in range(ranks // per):
        acc = inner_in[q * per]
        for j in range(1, per):
            acc = acc + inner_in[q * per + j]
        gates_ref[:, pl.ds(q * LANES, LANES)] = acc


def solution(mesh):
    groups, ranks = mesh.shape["grp"], mesh.shape["ep"]

    def on_device(tokens, grad_out, routes, route_weights, gate, up, down):
        count, feat = tokens.shape
        half, width = gate.shape[1:]
        rows = count // ranks
        far = groups // 4
        wide = width + LANES
        vmem = pl.BlockSpec(memory_space=pltpu.VMEM)
        hbm = pl.BlockSpec(memory_space=pl.ANY)
        dma = pltpu.SemaphoreType.DMA
        bf16, f32 = jnp.bfloat16, jnp.float32
        grad_tokens, grad_gates = pl.pallas_call(
            functools.partial(kernel, (groups, ranks, rows, width, half)),
            name="experts_backward",
            out_shape=(
                jax.ShapeDtypeStruct((count, feat), bf16),
                jax.ShapeDtypeStruct((2, count), f32),
            ),
            in_specs=[vmem, vmem, vmem, vmem, hbm, hbm, hbm],
            out_specs=(vmem, vmem),
            scratch_shapes=[
                pltpu.VMEM((far + 1, 2, 2, rows, wide), bf16),
                pltpu.VMEM((far + 1, 2, 2, rows, width), bf16),
                pltpu.VMEM((far + 1, 2, 2, rows, wide), bf16),
                pltpu.VMEM((far + 1, 2, rows, wide), bf16),
                pltpu.VMEM((far, rows, wide), bf16),
                pltpu.VMEM((far, rows, wide), bf16),
                pltpu.VMEM((far + 1, rows, wide), bf16),
                pltpu.VMEM((far + 1, rows, wide), bf16),
                pltpu.VMEM((rows, width), bf16),
                pltpu.VMEM((half, width), bf16),
                pltpu.VMEM((half, width), bf16),
                pltpu.VMEM((half, width), bf16),
                pltpu.VMEM((4 * rows, half), f32),
                pltpu.VMEM((4 * rows, half), f32),
                pltpu.VMEM((2, LANES), f32),
                pltpu.VMEM((ranks, 2, LANES), f32),
                dma((2, ranks)),
                dma((2, ranks)),
                dma((2, 2, far)),
                dma((2, 2, far + 1)),
                dma((2, 2, far + 1)),
                dma((2, 2, far + 1)),
                dma((2, far + 1)),
                dma((2, far + 1)),
                dma((2, 2, far + 1)),
                dma((2, 2, far + 1)),
                dma((2, ranks)),
                dma((2, ranks)),
                dma((3,)),
            ],
            compiler_params=pltpu.CompilerParams(
                collective_id=0, has_side_effects=True, vmem_limit_bytes=48 * 1024 * 1024
            ),
        )(tokens, grad_out, routes.T, route_weights.T, gate, up, down)
        return grad_tokens, grad_gates.T

    placed = (
        P("grp", "ep"),
        P("grp", "ep"),
        P("grp", None),
        P("grp", None),
        P("grp", None, None),
        P("grp", None, None),
        P("grp", None, None),
    )
    return jax.shard_map(
        on_device,
        mesh=mesh,
        in_specs=placed,
        out_specs=(P("grp", "ep"), P("grp", None)),
        check_vma=False,
    )
```

time: 466 us -> 116 us (0.25)
  the two profiles are of different devices: /device:TPU:64 before, /device:TPU:2 now
where the time goes in v1:
time: 116 us
  Pallas kernels  109 us (94%)
  local copies, waits for them, and re-layouts  6.31 us (5%)
    pallas_call x1, Pallas kernels, on_device(): pl.pallas_call(functools.partial(kernel, (groups, ranks, rows, width, hal...  109 us
    unnamed x12, local copies, waits for them, and re-layouts  6.31 us

profile of v1, /device:TPU:2, one launch (start us, length us, event | category | flops | bytes accessed | tf_op | source)
XLA Modules:
  0.0 115.7 jit_solution(9489845161079332474)
XLA Ops:
  0.6 0.0 copy-start
  0.6 1.9 %copy-done = bf16[1,384,4096]{2,1,0:T(8,128)(2,1)S(1)} copy-done((bf16[1,384,4096]{2,1,0:T(8,128)(2,1)S(1)}, bf16[1,384,4096]{2,1,0:T(8,128)(2,1)}, u32[]{:S(2)}) %copy-start) | copy-done | bytes 3145752
  2.5 0.0 copy-start.1
  2.5 0.9 copy-done.1
  3.4 0.0 copy-start.2
  3.4 0.9 copy-done.2
  4.3 0.0 copy-start.3
  4.3 0.7 copy-done.3
  5.0 0.0 copy-start.4
  5.0 0.7 copy-done.4
  5.7 108.8 %experts_backward.1 = (bf16[512,128]{1,0:T(8,128)(2,1)S(1)}, f32[2,512]{1,0:T(2,128)S(1)}) custom-call(bf16[512,128]{1,0:T(8,128)(2,1)S(1)} %copy-done.1, bf16[512,128]{1,0:T(8,128)(2,1)S(1)} %copy-done.2, s32[2,512]{1,0:T(2,128)S(1)} %bitcast.3, f32[2,512]{1,0:T(2,128)S(1)} %bitcast.4, bf16[1,384,4096]{2,1,0:T(8,128)(2,1)S(1)} %copy-done, ...), custom_call_target="tpu_custom_call" | custom-call | tf_op jit(solution)/shard_map/experts_backward/pallas_call | solution.py:477
  114.5 0.7 copy.11
  115.1 0.6 copy.12
Async XLA Ops:
  0.6 1.9 %copy-start = (bf16[1,384,4096]{2,1,0:T(8,128)(2,1)S(1)}, bf16[1,384,4096]{2,1,0:T(8,128)(2,1)}, u32[]{:S(2)}) copy-start(bf16[1,384,4096]{2,1,0:T(8,128)(2,1)} %gate_hbm.1) | copy-start | bytes 9437188
  2.5 0.9 copy-start.1
  3.4 0.9 copy-start.2
  4.3 0.7 copy-start.3
  5.0 0.7 copy-start.4

commit v2 on v1

--- a/solution.py
+++ b/solution.py
@@ -14,15 +14,19 @@
 
 def kernel(
     dims,
-    tok_ref,
-    grad_ref,
-    routes_ref,
-    rw_ref,
+    tok_hbm,
+    grad_hbm,
+    routes_hbm,
+    rw_hbm,
     gate_hbm,
     up_hbm,
     down_hbm,
     out_ref,
     gates_ref,
+    tok_ref,
+    grad_ref,
+    routes_ref,
+    rw_ref,
     xb,
     gb,
     cb,
@@ -52,6 +56,7 @@
     e_send,
     e_recv,
     w_sem,
+    i_sem,
 ):
     groups, ranks, rows, width, half = dims
     chips = groups // 2
@@ -68,15 +73,20 @@
     ahead = (right, left)
     expert = lax.rem(grp, experts)
     mid = width // 2
-    parts = (pl.ds(0, mid), pl.ds(mid, width + LANES - mid))
-
+    parts = (pl.ds(0, LANES + mid), pl.ds(LANES + mid, width - mid))
+
+    inputs = [
+        pltpu.make_async_copy(src, dst, i_sem.at[i])
+        for i, (src, dst) in enumerate(
+            ((routes_hbm, routes_ref), (rw_hbm, rw_ref), (tok_hbm, tok_ref), (grad_hbm, grad_ref))
+        )
+    ]
+    for copy in inputs:
+        copy.start()
     weights = [
         pltpu.make_async_copy(src.at[0], dst, w_sem.at[i])
         for i, (src, dst) in enumerate(((gate_hbm, wg), (up_hbm, wu), (down_hbm, wd)))
     ]
-    for copy in weights:
-        copy.start()
-
     barrier = pltpu.get_barrier_semaphore()
     for peer in (right, left, sibling):
         pl.semaphore_signal(barrier, inc=1, device_id=(peer, rank), device_id_type=MESH)
@@ -88,6 +98,10 @@
         return carry
 
     lax.fori_loop(1, ranks, greet, 0)
+    for copy in weights:
+        copy.start()
+    for copy in inputs:
+        copy.wait()
 
     token_lane = lax.broadcasted_iota(jnp.int32, (rows, rows * ranks), 1)
     token_row = lax.broadcasted_iota(jnp.int32, (rows, rows * ranks), 0)
@@ -108,12 +122,15 @@
         low = weight - high
         meta = meta + jnp.where(lane_f == chosen, high, 0.0)
         meta = meta + jnp.where(lane_f == chosen + float(experts), low, 0.0)
-    own_slot = (far, 1)
-    xb[far, 1, core, :, pl.ds(width, LANES)] = meta.astype(jnp.bfloat16)
+    xb[far, 1, core, :, pl.ds(0, LANES)] = meta.astype(jnp.bfloat16)
     own_rows = pl.ds(pl.multiple_of(rank * rows, rows), rows)
-    own_cols = pl.ds(pl.multiple_of(rank * LANES, LANES), LANES)
-    xb[far, 1, core, :, own_cols] = tok_ref[own_rows, :]
-    gb[far, 1, core, :, own_cols] = grad_ref[own_rows, :]
+
+    def features(which, owner):
+        shift = LANES if which == 0 else 0
+        return pl.ds(pl.multiple_of(owner * LANES + shift, LANES), LANES)
+
+    xb[far, 1, core, :, features(0, rank)] = tok_ref[own_rows, :]
+    gb[far, 1, core, :, features(1, rank)] = grad_ref[own_rows, :]
 
     pl.semaphore_wait(barrier, 3 + ranks - 1)
 
@@ -122,7 +139,7 @@
         peer = lax.rem(rank + i, ranks)
         return pltpu.make_async_remote_copy(
             src_ref=src.at[pl.ds(pl.multiple_of(peer * rows, rows), rows), :],
-            dst_ref=buf.at[far, 1, core, :, own_cols],
+            dst_ref=buf.at[far, 1, core, :, features(which, rank)],
             send_sem=a_send.at[which, i],
             recv_sem=a_recv.at[which, i],
             device_id=(grp, peer),
@@ -132,7 +149,7 @@
     def landed(which, i):
         buf = (xb, gb)[which]
         peer = lax.rem(rank + ranks - i, ranks)
-        here = buf.at[far, 1, core, :, pl.ds(pl.multiple_of(peer * LANES, LANES), LANES)]
+        here = buf.at[far, 1, core, :, features(which, peer)]
         return pltpu.make_async_remote_copy(
             src_ref=here,
             dst_ref=here,
@@ -158,7 +175,7 @@
             src = buf.at[step, direction, core]
         return pltpu.make_async_remote_copy(
             src_ref=src,
-            dst_ref=buf.at[step + 1, direction if not (isinstance(step, int) and step == far - 1) else 0, core],
+            dst_ref=buf.at[step + 1, direction, core],
             send_sem=g_send.at[direction, which, step],
             recv_sem=g_recv.at[direction, which, step + 1],
             device_id=(ahead[direction], rank),
@@ -217,7 +234,7 @@
     def first_half(slot):
         for side in range(2):
             shared(0, slot, side).wait_recv()
-        x = xb[slot, :, :, :, pl.ds(0, width)].reshape(4 * rows, width)
+        x = xb[slot, :, :, :, pl.ds(LANES, width)].reshape(4 * rows, width)
         gate_s[...] = lax.dot_general(x, wg[...], NT, preferred_element_type=jnp.float32)
         up_s[...] = lax.dot_general(x, wu[...], NT, preferred_element_type=jnp.float32)
 
@@ -244,14 +261,14 @@
         inner = jnp.sum(hidden * back, axis=1, keepdims=True)
         d_gate = (back * up_pre * sig * (1.0 + gate_pre * (1.0 - sig))).astype(jnp.bfloat16)
         d_up = (back * active).astype(jnp.bfloat16)
-        info = xb[slot, :, :, :, pl.ds(width, LANES)].reshape(4 * rows, LANES).astype(jnp.float32)
+        info = xb[slot, :, :, :, pl.ds(0, LANES)].reshape(4 * rows, LANES).astype(jnp.float32)
         picked = (lanes_m == expert) | (lanes_m == expert + experts)
         weight = jnp.sum(jnp.where(picked, info, 0.0), axis=1, keepdims=True)
         inner = jnp.where(weight > 0.0, inner, 0.0)
         high = inner.astype(jnp.bfloat16).astype(jnp.float32)
         low = inner - high
         extra = jnp.where(lanes_m == grp, high, jnp.where(lanes_m == grp + groups, low, 0.0))
-        cb[slot, :, :, :, pl.ds(width, LANES)] = extra.astype(jnp.bfloat16).reshape(
+        cb[slot, :, :, :, pl.ds(0, LANES)] = extra.astype(jnp.bfloat16).reshape(
             2, 2, rows, LANES
         )
         tile = 512
@@ -260,7 +277,8 @@
             cols = pl.ds(pl.multiple_of(n * tile, tile), tile)
             part = jnp.dot(d_gate, wg[:, cols], preferred_element_type=jnp.float32)
             part = part + jnp.dot(d_up, wu[:, cols], preferred_element_type=jnp.float32)
-            cb[slot, :, :, :, cols] = (weight * part).astype(jnp.bfloat16).reshape(
+            shifted = pl.ds(pl.multiple_of(n * tile + LANES, LANES), tile)
+            cb[slot, :, :, :, shifted] = (weight * part).astype(jnp.bfloat16).reshape(
                 2, 2, rows, tile
             )
             return carry
@@ -269,32 +287,44 @@
         for side in range(2):
             hand_over(slot, side).start()
 
+    def pass_on(t, which):
+        for direction in range(2):
+            ring(direction, which, t - 1).wait_recv()
+
+        @pl.when(t < far - 1)
+        def _():
+            for direction in range(2):
+                ring(direction, which, t).start()
+
+        @pl.when(t == far - 1)
+        def _():
+            ring_last(which, which).start()
+
+        for direction in range(2):
+            share(which, t, direction).start()
+
     def step(t, carry):
-        for which in range(2):
-
-            @pl.when(t < far)
-            def _():
-                for direction in range(2):
-                    ring(direction, which, t - 1).wait_recv()
-                    share(which, t, direction).start()
-
-            @pl.when(t < far - 1)
-            def _():
-                for direction in range(2):
-                    ring(direction, which, t).start()
-
-            @pl.when(t == far - 1)
-            def _():
-                ring_last(which, which).start()
-
-            @pl.when(t == far)
-            def _():
+        @pl.when(t < far)
+        def _():
+            pass_on(t, 0)
+
+        @pl.when(t > 1)
+        def _():
+            second_half(t - 1)
+
+        @pl.when(t < far)
+        def _():
+            pass_on(t, 1)
+
+        @pl.when(t == far)
+        def _():
+            for which in range(2):
                 ring_last(which, which).wait_recv()
                 share(which, far, 0).start()
 
-            @pl.when(t > 1)
-            def _():
-                (first_half, second_half)[which](t - 1)
+        @pl.when(t < far + 1)
+        def _():
+            first_half(t)
 
         return carry
 
@@ -339,51 +369,51 @@
 
     hand_over(far, 1).wait_recv()
 
-    def leave(i):
-        peer = lax.rem(rank + i, ranks)
-        return pltpu.make_async_remote_copy(
-            src_ref=fin.at[:, pl.ds(pl.multiple_of(peer * LANES, LANES), LANES)],
+    def leave(peer):
+        return pltpu.make_async_remote_copy(
+            src_ref=fin.at[:, features(0, peer)],
             dst_ref=out_ref.at[own_rows, :],
-            send_sem=e_send.at[0, i],
-            recv_sem=e_recv.at[0, i],
+            send_sem=e_send.at[0, peer],
+            recv_sem=e_recv.at[0, rank],
             device_id=(grp, peer),
             device_id_type=MESH,
         )
 
-    def leave_inner(i):
-        peer = lax.rem(rank + i, ranks)
+    def leave_inner(peer):
         return pltpu.make_async_remote_copy(
             src_ref=inner_out,
             dst_ref=inner_in.at[rank],
-            send_sem=e_send.at[1, i],
-            recv_sem=e_recv.at[1, i],
+            send_sem=e_send.at[1, peer],
+            recv_sem=e_recv.at[1, rank],
             device_id=(grp, peer),
             device_id_type=MESH,
         )
 
-    def back_home(i):
-        peer = lax.rem(rank + ranks - i, ranks)
+    def back_home(peer):
         here = out_ref.at[pl.ds(pl.multiple_of(peer * rows, rows), rows), :]
         return pltpu.make_async_remote_copy(
             src_ref=here,
             dst_ref=here,
-            send_sem=e_send.at[0, i],
-            recv_sem=e_recv.at[0, i],
+            send_sem=e_send.at[0, peer],
+            recv_sem=e_recv.at[0, peer],
             device_id=(grp, peer),
             device_id_type=MESH,
         )
 
-    def back_home_inner(i):
-        peer = lax.rem(rank + ranks - i, ranks)
+    def back_home_inner(peer):
         return pltpu.make_async_remote_copy(
             src_ref=inner_out,
             dst_ref=inner_in.at[peer],
-            send_sem=e_send.at[1, i],
-            recv_sem=e_recv.at[1, i],
+            send_sem=e_send.at[1, peer],
+            recv_sem=e_recv.at[1, peer],
             device_id=(grp, peer),
             device_id_type=MESH,
         )
 
+    place = lane == lax.rem(rank, LANES // rows) * rows + lax.broadcasted_iota(
+        jnp.int32, (rows, LANES), 0
+    )
+    share_of = ranks // 2
     for part in range(2):
         cols = parts[part]
         for direction in range(2):
@@ -393,32 +423,43 @@
             + rl[0, :, cols].astype(jnp.float32)
             + rr[0, :, cols].astype(jnp.float32)
         )
+        fin[:, cols] = total.astype(jnp.bfloat16)
+
+        def send_out(i, carry):
+            peer = part * share_of + lax.rem(rank + i, share_of)
+
+            @pl.when(peer != rank)
+            def _():
+                leave(peer).start()
+
+            return carry
+
+        lax.fori_loop(0, share_of, send_out, 0)
         if part == 0:
-            fin[:, pl.ds(0, mid)] = total.astype(jnp.bfloat16)
-        else:
-            fin[:, pl.ds(mid, width - mid)] = total[:, : width - mid].astype(jnp.bfloat16)
-            inner_lanes = total[:, width - mid :]
-
-    place = (lane == lax.rem(rank, LANES // rows) * rows + lax.broadcasted_iota(
-        jnp.int32, (rows, LANES), 0
-    ))
-    for k in range(2):
-        chosen = column(routes_f, k)
-        wanted = jnp.zeros((rows, LANES), jnp.bool_)
-        for piece in range(4):
-            wanted = wanted | (lane_f == chosen + float(piece * experts))
-        gate_grad = jnp.sum(jnp.where(wanted, inner_lanes, 0.0), axis=1, keepdims=True)
-        inner_out[k : k + 1, :] = jnp.sum(jnp.where(place, gate_grad, 0.0), axis=0, keepdims=True)
-
-    def send_out(i, carry):
-        leave(i).start()
-        leave_inner(i).start()
-        return carry
-
-    lax.fori_loop(1, ranks, send_out, 0)
-    out_ref[own_rows, :] = fin[:, own_cols]
+            inner_lanes = total[:, :LANES]
+            for k in range(2):
+                chosen = column(routes_f, k)
+                wanted = jnp.zeros((rows, LANES), jnp.bool_)
+                for piece in range(4):
+                    wanted = wanted | (lane_f == chosen + float(piece * experts))
+                gate_grad = jnp.sum(jnp.where(wanted, inner_lanes, 0.0), axis=1, keepdims=True)
+                inner_out[k : k + 1, :] = jnp.sum(
+                    jnp.where(place, gate_grad, 0.0), axis=0, keepdims=True
+                )
+
+            def send_inner(i, carry):
+                leave_inner(lax.rem(rank + i, ranks)).start()
+                return carry
+
+            lax.fori_loop(1, ranks, send_inner, 0)
+
+    stay = pltpu.make_async_copy(
+        fin.at[:, features(0, rank)], out_ref.at[own_rows, :], i_sem.at[4]
+    )
+    stay.start()
     inner_in[rank] = inner_out[...]
 
+    stay.wait()
     def drain_in(i, carry):
         for which in range(2):
             enter(which, i).wait_send()
@@ -446,10 +487,11 @@
                 returning(direction, part, distance).wait_send()
 
     def finish(i, carry):
-        back_home(i).wait_recv()
-        back_home_inner(i).wait_recv()
-        leave(i).wait_send()
-        leave_inner(i).wait_send()
+        peer = lax.rem(rank + i, ranks)
+        back_home(peer).wait_recv()
+        back_home_inner(peer).wait_recv()
+        leave(peer).wait_send()
+        leave_inner(peer).wait_send()
         return carry
 
     lax.fori_loop(1, ranks, finish, 0)
@@ -471,7 +513,7 @@
         far = groups // 4
         wide = width + LANES
         vmem = pl.BlockSpec(memory_space=pltpu.VMEM)
-        hbm = pl.BlockSpec(memory_space=pl.ANY)
+        hbm = pl.BlockSpec(memory_space=pltpu.HBM)
         dma = pltpu.SemaphoreType.DMA
         bf16, f32 = jnp.bfloat16, jnp.float32
         grad_tokens, grad_gates = pl.pallas_call(
@@ -481,9 +523,13 @@
                 jax.ShapeDtypeStruct((count, feat), bf16),
                 jax.ShapeDtypeStruct((2, count), f32),
             ),
-            in_specs=[vmem, vmem, vmem, vmem, hbm, hbm, hbm],
-            out_specs=(vmem, vmem),
+            in_specs=[hbm] * 7,
+            out_specs=(hbm, vmem),
             scratch_shapes=[
+                pltpu.VMEM((count, feat), bf16),
+                pltpu.VMEM((count, feat), bf16),
+                pltpu.VMEM((2, count), jnp.int32),
+                pltpu.VMEM((2, count), f32),
                 pltpu.VMEM((far + 1, 2, 2, rows, wide), bf16),
                 pltpu.VMEM((far + 1, 2, 2, rows, width), bf16),
                 pltpu.VMEM((far + 1, 2, 2, rows, wide), bf16),
@@ -492,7 +538,7 @@
                 pltpu.VMEM((far, rows, wide), bf16),
                 pltpu.VMEM((far + 1, rows, wide), bf16),
                 pltpu.VMEM((far + 1, rows, wide), bf16),
-                pltpu.VMEM((rows, width), bf16),
+                pltpu.VMEM((rows, wide), bf16),
                 pltpu.VMEM((half, width), bf16),
                 pltpu.VMEM((half, width), bf16),
                 pltpu.VMEM((half, width), bf16),
@@ -513,9 +559,10 @@
                 dma((2, ranks)),
                 dma((2, ranks)),
                 dma((3,)),
+                dma((5,)),
             ],
             compiler_params=pltpu.CompilerParams(
-                collective_id=0, has_side_effects=True, vmem_limit_bytes=48 * 1024 * 1024
+                collective_id=0, has_side_effects=True, vmem_limit_bytes=67043328
             ),
         )(tokens, grad_out, routes.T, route_weights.T, gate, up, down)
         return grad_tokens, grad_gates.T

time: 116 us -> 111 us (0.957)
  the two profiles are of different devices: /device:TPU:2 before, /device:TPU:8 now
where the time goes in v2:
time: 111 us
  Pallas kernels  108 us (97%)
  local copies, waits for them, and re-layouts  2.85 us (3%)
    pallas_call x1, Pallas kernels, on_device(): pl.pallas_call(functools.partial(kernel, (groups, ranks, rows, width, hal...  108 us
    unnamed x2, local copies, waits for them, and re-layouts  2.85 us

profile of v2, /device:TPU:8, one launch (start us, length us, event | category | flops | bytes accessed | tf_op | source)
XLA Modules:
  0.0 111.2 jit_solution(6183234195325516935)
XLA Ops:
  0.6 107.7 %experts_backward.1 = (bf16[512,128]{1,0:T(8,128)(2,1)}, f32[2,512]{1,0:T(2,128)}) custom-call(bf16[512,128]{1,0:T(8,128)(2,1)} %tok_hbm.1, bf16[512,128]{1,0:T(8,128)(2,1)} %grad_hbm.1, s32[2,512]{1,0:T(2,128)} %bitcast.3, f32[2,512]{1,0:T(2,128)} %bitcast.4, bf16[1,384,4096]{2,1,0:T(8,128)(2,1)} %gate_hbm.1, bf16[1,384,4096]{2,1,0:T(8,128)(2,1)} %up_hbm.1, ...), custom_call_target="tpu_custom_call" | custom-call | tf_op jit(solution)/shard_map/experts_backward/pallas_call | solution.py:519
  108.4 1.6 %copy.11 = bf16[512,128]{1,0:T(8,128)(2,1)} copy(bf16[512,128]{1,0:T(8,128)(2,1)} %get-tuple-element.8) | data formatting | bytes 262144
  109.9 1.3 %copy.12 = f32[512,2]{0,1:T(2,128)} copy(f32[512,2]{0,1:T(2,128)} %bitcast.5) | data formatting | bytes 8192

commit v3 on v2

--- a/solution.py
+++ b/solution.py
@@ -9,6 +9,7 @@
 
 MESH = pl.DeviceIdType.MESH
 LANES = 128
+PARTS = 4
 NT = (((1,), (1,)), ((), ()))
 
 
@@ -36,11 +37,9 @@
     tl,
     tr,
     fin,
-    wg,
-    wu,
+    wgu,
     wd,
-    gate_s,
-    up_s,
+    pre_s,
     inner_out,
     inner_in,
     a_send,
@@ -72,8 +71,13 @@
     sibling = z * 2 + other
     ahead = (right, left)
     expert = lax.rem(grp, experts)
-    mid = width // 2
-    parts = (pl.ds(0, LANES + mid), pl.ds(LANES + mid, width - mid))
+    piece = width // PARTS
+    parts = [pl.ds(0, LANES + piece)]
+    parts += [pl.ds(LANES + p * piece, piece) for p in range(1, PARTS)]
+    order = [
+        [p for p in range(PARTS) if p % 2 != d] + [p for p in range(PARTS) if p % 2 == d]
+        for d in range(2)
+    ]
 
     inputs = [
         pltpu.make_async_copy(src, dst, i_sem.at[i])
@@ -85,7 +89,13 @@
         copy.start()
     weights = [
         pltpu.make_async_copy(src.at[0], dst, w_sem.at[i])
-        for i, (src, dst) in enumerate(((gate_hbm, wg), (up_hbm, wu), (down_hbm, wd)))
+        for i, (src, dst) in enumerate(
+            (
+                (gate_hbm, wgu.at[pl.ds(0, half), :]),
+                (up_hbm, wgu.at[pl.ds(half, half), :]),
+                (down_hbm, wd),
+            )
+        )
     ]
     barrier = pltpu.get_barrier_semaphore()
     for peer in (right, left, sibling):
@@ -235,15 +245,14 @@
         for side in range(2):
             shared(0, slot, side).wait_recv()
         x = xb[slot, :, :, :, pl.ds(LANES, width)].reshape(4 * rows, width)
-        gate_s[...] = lax.dot_general(x, wg[...], NT, preferred_element_type=jnp.float32)
-        up_s[...] = lax.dot_general(x, wu[...], NT, preferred_element_type=jnp.float32)
-
-    def hand_over(slot, side):
-        return pltpu.make_async_remote_copy(
-            src_ref=cb.at[slot, side, other],
-            dst_ref=sb.at[slot, side],
-            send_sem=c_send.at[side, slot],
-            recv_sem=c_recv.at[side, slot],
+        pre_s[...] = lax.dot_general(x, wgu[...], NT, preferred_element_type=jnp.float32)
+
+    def hand_over(slot, side, part):
+        return pltpu.make_async_remote_copy(
+            src_ref=cb.at[slot, side, other, :, parts[part]],
+            dst_ref=sb.at[slot, side, :, parts[part]],
+            send_sem=c_send.at[side, part, slot],
+            recv_sem=c_recv.at[side, part, slot],
             device_id=(sibling, rank),
             device_id_type=MESH,
         )
@@ -253,8 +262,8 @@
             shared(1, slot, side).wait_recv()
         gr = gb[slot].reshape(4 * rows, width)
         back = lax.dot_general(gr, wd[...], NT, preferred_element_type=jnp.float32)
-        gate_pre = gate_s[...]
-        up_pre = up_s[...]
+        gate_pre = pre_s[:, pl.ds(0, half)]
+        up_pre = pre_s[:, pl.ds(half, half)]
         sig = jax.nn.sigmoid(gate_pre)
         active = gate_pre * sig
         hidden = (active * up_pre).astype(jnp.bfloat16).astype(jnp.float32)
@@ -271,21 +280,16 @@
         cb[slot, :, :, :, pl.ds(0, LANES)] = extra.astype(jnp.bfloat16).reshape(
             2, 2, rows, LANES
         )
-        tile = 512
-
-        def columns(n, carry):
-            cols = pl.ds(pl.multiple_of(n * tile, tile), tile)
-            part = jnp.dot(d_gate, wg[:, cols], preferred_element_type=jnp.float32)
-            part = part + jnp.dot(d_up, wu[:, cols], preferred_element_type=jnp.float32)
-            shifted = pl.ds(pl.multiple_of(n * tile + LANES, LANES), tile)
-            cb[slot, :, :, :, shifted] = (weight * part).astype(jnp.bfloat16).reshape(
-                2, 2, rows, tile
+        d_both = jnp.concatenate([d_gate, d_up], axis=1)
+        for p in range(PARTS):
+            part = jnp.dot(
+                d_both, wgu[:, pl.ds(p * piece, piece)], preferred_element_type=jnp.float32
             )
-            return carry
-
-        lax.fori_loop(0, width // tile, columns, 0)
-        for side in range(2):
-            hand_over(slot, side).start()
+            cb[slot, :, :, :, pl.ds(LANES + p * piece, piece)] = (
+                (weight * part).astype(jnp.bfloat16).reshape(2, 2, rows, piece)
+            )
+            for side in range(2):
+                hand_over(slot, side, p).start()
 
     def pass_on(t, which):
         for direction in range(2):
@@ -346,28 +350,26 @@
             jnp.float32
         )
 
-    hand_over(far, 0).wait_recv()
-    for direction in range(2):
+    for part in range(PARTS):
+        direction = part % 2
         stage = (tl, tr)[direction]
-        cols = parts[direction]
+        cols = parts[part]
+        hand_over(far, 0, part).wait_recv()
         stage[far, :, cols] = own_terms(far, 0, cols).astype(jnp.bfloat16)
-        returning(direction, direction, far).start()
+        returning(direction, part, far).start()
     for distance in range(far - 1, 0, -1):
-        for direction in range(2):
-            hand_over(distance, direction).wait_recv()
-        for nth in range(2):
+        for nth in range(PARTS):
             for direction in range(2):
                 stage, land = ((tl, rl), (tr, rr))[direction]
-                part = nth if distance < far - 1 else (nth + 1 - direction) % 2
+                part = order[direction][nth]
                 cols = parts[part]
+                hand_over(distance, direction, part).wait_recv()
                 value = own_terms(distance, direction, cols)
-                if distance < far - 1 or part == direction:
+                if distance < far - 1 or part % 2 == direction:
                     returning(direction, part, distance + 1).wait_recv()
                     value = value + land[distance, :, cols].astype(jnp.float32)
                 stage[distance, :, cols] = value.astype(jnp.bfloat16)
                 returning(direction, part, distance).start()
-
-    hand_over(far, 1).wait_recv()
 
     def leave(peer):
         return pltpu.make_async_remote_copy(
@@ -413,9 +415,10 @@
     place = lane == lax.rem(rank, LANES // rows) * rows + lax.broadcasted_iota(
         jnp.int32, (rows, LANES), 0
     )
-    share_of = ranks // 2
-    for part in range(2):
+    share_of = ranks // PARTS
+    for part in range(PARTS):
         cols = parts[part]
+        hand_over(far, 1, part).wait_recv()
         for direction in range(2):
             returning(direction, part, 1).wait_recv()
         total = (
@@ -479,10 +482,12 @@
                     ring(direction, which, slot).wait_send()
     for slot in range(1, far + 1):
         for side in range(2):
-            hand_over(slot, side).wait_send()
+            for part in range(PARTS):
+                hand_over(slot, side, part).wait_send()
     for direction in range(2):
-        returning(direction, direction, far).wait_send()
-        for part in range(2):
+        for part in range(PARTS):
+            if part % 2 == direction:
+                returning(direction, part, far).wait_send()
             for distance in range(1, far):
                 returning(direction, part, distance).wait_send()
 
@@ -539,11 +544,9 @@
                 pltpu.VMEM((far + 1, rows, wide), bf16),
                 pltpu.VMEM((far + 1, rows, wide), bf16),
                 pltpu.VMEM((rows, wide), bf16),
+                pltpu.VMEM((2 * half, width), bf16),
                 pltpu.VMEM((half, width), bf16),
-                pltpu.VMEM((half, width), bf16),
-                pltpu.VMEM((half, width), bf16),
-                pltpu.VMEM((4 * rows, half), f32),
-                pltpu.VMEM((4 * rows, half), f32),
+                pltpu.VMEM((4 * rows, 2 * half), f32),
                 pltpu.VMEM((2, LANES), f32),
                 pltpu.VMEM((ranks, 2, LANES), f32),
                 dma((2, ranks)),
@@ -552,10 +555,10 @@
                 dma((2, 2, far + 1)),
                 dma((2, 2, far + 1)),
                 dma((2, 2, far + 1)),
-                dma((2, far + 1)),
-                dma((2, far + 1)),
-                dma((2, 2, far + 1)),
-                dma((2, 2, far + 1)),
+                dma((2, PARTS, far + 1)),
+                dma((2, PARTS, far + 1)),
+                dma((2, PARTS, far + 1)),
+                dma((2, PARTS, far + 1)),
                 dma((2, ranks)),
                 dma((2, ranks)),
                 dma((3,)),

time: 111 us -> 106 us (0.955)
  Pallas kernels: 108 us -> 103 us
    pallas_call x1, Pallas kernels: 108 us -> 103 us  [on_device(): pl.pallas_call(functools.partial(kernel, (groups, ranks, rows, width, hal...]
where the time goes in v3:
time: 106 us
  Pallas kernels  103 us (97%)
  local copies, waits for them, and re-layouts  2.85 us (3%)
    pallas_call x1, Pallas kernels, on_device(): pl.pallas_call(functools.partial(kernel, (groups, ranks, rows, width, hal...  103 us
    unnamed x2, local copies, waits for them, and re-layouts  2.85 us

profile of v3, /device:TPU:8, one launch (start us, length us, event | category | flops | bytes accessed | tf_op | source)
XLA Modules:
  0.0 106.2 jit_solution(14331822341129960344)
XLA Ops:
  0.6 102.7 %experts_backward.1 = (bf16[512,128]{1,0:T(8,128)(2,1)}, f32[2,512]{1,0:T(2,128)}) custom-call(bf16[512,128]{1,0:T(8,128)(2,1)} %tok_hbm.1, bf16[512,128]{1,0:T(8,128)(2,1)} %grad_hbm.1, s32[2,512]{1,0:T(2,128)} %bitcast.3, f32[2,512]{1,0:T(2,128)} %bitcast.4, bf16[1,384,4096]{2,1,0:T(8,128)(2,1)} %gate_hbm.1, bf16[1,384,4096]{2,1,0:T(8,128)(2,1)} %up_hbm.1, ...), custom_call_target="tpu_custom_call" | custom-call | tf_op jit(solution)/shard_map/experts_backward/pallas_call | solution.py:524
  103.3 1.6 %copy.11 = bf16[512,128]{1,0:T(8,128)(2,1)} copy(bf16[512,128]{1,0:T(8,128)(2,1)} %get-tuple-element.8) | data formatting | bytes 262144
  104.9 1.3 %copy.12 = f32[512,2]{0,1:T(2,128)} copy(f32[512,2]{0,1:T(2,128)} %bitcast.5) | data formatting | bytes 8192

commit v4 on v3

--- a/solution.py
+++ b/solution.py
@@ -508,6 +508,19 @@
         gates_ref[:, pl.ds(q * LANES, LANES)] = acc
 
 
+def settle(rows_ref, gates_ref, rows_out, gates_out, rows_v, gates_v, sem):
+    pairs = ((gates_ref, gates_v, gates_out), (rows_ref, rows_v, rows_out))
+    reads = [pltpu.make_async_copy(a, b, sem.at[0, i]) for i, (a, b, c) in enumerate(pairs)]
+    writes = [pltpu.make_async_copy(b, c, sem.at[1, i]) for i, (a, b, c) in enumerate(pairs)]
+    for read in reads:
+        read.start()
+    for read, write in zip(reads, writes):
+        read.wait()
+        write.start()
+    for write in writes:
+        write.wait()
+
+
 def solution(mesh):
     groups, ranks = mesh.shape["grp"], mesh.shape["ep"]
 
@@ -568,6 +581,22 @@
                 collective_id=0, has_side_effects=True, vmem_limit_bytes=67043328
             ),
         )(tokens, grad_out, routes.T, route_weights.T, gate, up, down)
+        grad_tokens, grad_gates = pl.pallas_call(
+            settle,
+            name="settle",
+            out_shape=(
+                jax.ShapeDtypeStruct((count, feat), bf16),
+                jax.ShapeDtypeStruct((2, count), f32),
+            ),
+            in_specs=[hbm, hbm],
+            out_specs=(hbm, hbm),
+            scratch_shapes=[
+                pltpu.VMEM((count, feat), bf16),
+                pltpu.VMEM((2, count), f32),
+                dma((2, 2)),
+            ],
+            compiler_params=pltpu.CompilerParams(vmem_limit_bytes=67043328),
+        )(grad_tokens, grad_gates)
         return grad_tokens, grad_gates.T
 
     placed = (

time: 106 us -> 105 us (level)
  local copies, waits for them, and re-layouts: 2.85 us -> 0 us
    unnamed x2 -> x0, local copies, waits for them, and re-layouts: 2.85 us -> none
    pallas_call x0 -> x1, Pallas kernels: none -> 1.6 us  [on_device(): pl.pallas_call(settle, name='settle', out_shape=(jax.ShapeDtypeStruct((co...]
where the time goes in v4:
time: 105 us
  Pallas kernels  104 us (99%)
    pallas_call x1, Pallas kernels, on_device(): pl.pallas_call(functools.partial(kernel, (groups, ranks, rows, width, hal...  103 us

profile of v4, /device:TPU:8, one launch (start us, length us, event | category | flops | bytes accessed | tf_op | source)
XLA Modules:
  0.0 104.9 jit_solution(16729653114919727121)
XLA Ops:
  0.6 102.7 %experts_backward.1 = (bf16[512,128]{1,0:T(8,128)(2,1)}, f32[2,512]{1,0:T(2,128)}) custom-call(bf16[512,128]{1,0:T(8,128)(2,1)} %tok_hbm.1, bf16[512,128]{1,0:T(8,128)(2,1)} %grad_hbm.1, s32[2,512]{1,0:T(2,128)} %bitcast.3, f32[2,512]{1,0:T(2,128)} %bitcast.4, bf16[1,384,4096]{2,1,0:T(8,128)(2,1)} %gate_hbm.1, bf16[1,384,4096]{2,1,0:T(8,128)(2,1)} %up_hbm.1, ...), custom_call_target="tpu_custom_call" | custom-call | tf_op jit(solution)/shard_map/experts_backward/pallas_call | solution.py:537
  103.3 1.6 %settle.1 = (bf16[512,128]{1,0:T(8,128)(2,1)}, f32[2,512]{1,0:T(2,128)}) custom-call(bf16[512,128]{1,0:T(8,128)(2,1)} %get-tuple-element.6.rows_ref, f32[2,512]{1,0:T(2,128)} %get-tuple-element.7.gates_ref), custom_call_target="tpu_custom_call" | custom-call | tf_op jit(solution)/shard_map/settle/pallas_call | solution.py:584
